TPU v7x, 32 devices: a whole 2x2x4 slice. The times are simulated.
32 devices in a mesh: groups: 2 (over y), feat: 8 (over z, x), corp: 2 (over core).
Axes of the slice: x: 2, y: 2, z: 4, core: 2. Of those that a mesh axis runs over, the one named last changes fastest.
Arguments:
- query_features: bfloat16 [1536, 16384], P(('groups', 'corp'), 'feat'), parts along dimension 0, may hold values from -6 to 6
- inverse_kernel: bfloat16 [16384, 16384], P(None, 'feat'), may hold values from -1 to 3, as said below
- doc_features: bfloat16 [512, 16384], P(('groups', 'corp'), 'feat'), parts along dimension 0, may hold values from -0.046875 to 0.046875
Outputs:
- scores: float32 [1536, 256], P(('groups', 'feat'), 'corp'), parts along dimension 0
There are 2 independent parts, one for each index of `groups`. A program takes and returns all parts, laid end to end along the dimension named above; an argument that names none is the same for every part. Nothing has to cross between parts.
Inputs may be any that keep to these rules, and one draw needn't show every extreme that they name: inverse_kernel is symmetric.
All inputs are finite; a program needn't handle non-finite values.
Results may differ from a plain program's by a relative error of at most 0.0003.
Values may be sent and summed in bfloat16 or wider, within the bound.
No kernel may reach another device: no remote copies, remote signals or barrier semaphores. Data moves between devices by JAX's collectives and lax.ppermute only.
A program may use at most 128 MiB of HBM per device.

v0:
```python
import jax
import jax.numpy as jnp
from jax import lax
from jax.sharding import PartitionSpec as P


def on_device(query_features, inverse_kernel, doc_features):
    applied = jnp.dot(
        lax.all_gather(doc_features, "feat", axis=1, tiled=True),
        inverse_kernel,
        preferred_element_type=jnp.float32,
    )
    left_rows = lax.all_gather(query_features, "corp", axis=0, tiled=True).astype(jnp.float32)
    return lax.psum_scatter(
        lax.dot_general(
            left_rows,
            applied,
            (((1,), (1,)), ((), ())),
            precision=lax.Precision.HIGHEST,
            preferred_element_type=jnp.float32,
        ),
        "feat",
        scatter_dimension=0,
        tiled=True,
    )


def solution(mesh):
    placed = (P(("groups", "corp"), "feat"), P(None, "feat"), P(("groups", "corp"), "feat"))
    return jax.shard_map(
        on_device,
        mesh=mesh,
        in_specs=placed,
        out_specs=P(("groups", "feat"), "corp"),
        check_vma=False,
    )
```

profile of v0, /device:TPU:0, one launch (start us, length us, event | category | flops | bytes accessed | tf_op | source)
XLA Modules:
  0.0 184.1 jit_solution(11617538823632090180)
XLA Ops:
  6.5 0.0 all-gather.3.cloned.1.call-start
  6.5 0.7 all-gather.3.cloned.1.call-update
  7.3 0.0 all-gather.5.cloned.1.call-start
  7.3 0.7 all-gather.5.cloned.1.call-update
  8.0 0.0 reduce-scatter.4.cloned.1.call-start
  8.1 77.0 %all-gather.3.cloned.1.call-done = bf16[128,16384]{1,0:T(8,128)(2,1)} async-done(((bf16[128,2048]{1,0:T(8,128)(2,1)}), bf16[128,16384]{1,0:T(8,128)(2,1)}) %all-gather.3.cloned.1.call-update) | async-done | bytes 4194320 | tf_op jit(solution)/shard_map/all_gather | solution.py:9
  85.0 25.5 %fusion = f32[128,2048]{1,0:T(8,128)S(1)} fusion(bf16[128,16384]{1,0:T(8,128)(2,1)} %all-gather.3.cloned.1.call-done, bf16[16384,2048]{1,0:T(8,128)(2,1)} %param.4), kind=kOutput, calls=%fused_computation.1 | convolution fusion | flops 8589934592 | bytes 72351744 | tf_op jit(solution)/shard_map/dot_general | solution.py:8
  110.6 0.0 all-gather.5.cloned.1.call-done
  110.6 5.1 %convolution_bitcast_fusion = f32[768,128]{0,1:T(8,128)S(1)} fusion(f32[128,2048]{1,0:T(8,128)S(1)} %fusion, bf16[768,2048]{1,0:T(8,128)(2,1)} %all-gather.5.cloned.1.call-done), kind=kOutput, calls=%fused_computation | convolution fusion | flops 2415919104 | bytes 4587520 | tf_op jit(solution)/shard_map/dot_general | solution.py:15
  115.7 0.9 copy.6
  116.6 0.0 reduce-scatter.4.cloned.1.call-update
  116.6 60.9 %reduce-scatter.4.cloned.1.call-done = f32[96,128]{1,0:T(8,128)} async-done(((f32[768,128]{1,0:T(8,128)}), f32[96,128]{1,0:T(8,128)}) %reduce-scatter.4.cloned.1.call-update) | async-done | bytes 49168 | tf_op jit(solution)/shard_map/reduce_scatter | solution.py:14
Async XLA Ops:
  6.5 78.5 %all-gather.3.cloned.1.call-start = ((), (), s32[]{:S(2)}) async-start(), calls=%async_computation.1 | async-start | bytes 4718592 | tf_op jit(solution)/shard_map/all_gather | solution.py:9
  7.3 103.3 %all-gather.5.cloned.1.call-start = ((), (), s32[]{:S(2)}) async-start(), calls=%async_computation.2 | async-start | bytes 4718592 | tf_op jit(solution)/shard_map/all_gather | solution.py:13
  8.0 169.6 %reduce-scatter.4.cloned.1.call-start = ((), (), s32[]{:S(2)}) async-start(), calls=%async_computation.3 | async-start | bytes 442368 | tf_op jit(solution)/shard_map/reduce_scatter | solution.py:14
Sparse Core Ops, SparseCore 0:
  9.5 75.4 all-gather.2
  86.6 10.6 all-gather.4
  116.7 60.7 reduce-scatter.3
where the time goes:
time: 184 us
  waiting for transfers between devices  139 us (76%)
  matrix products  30.6 us (17%)
  between operations  13.1 us (7%)
    all_gather x1, waiting for transfers between devices, on_device(): lax.all_gather(doc_features, 'feat', axis=1, tiled=True)  77 us
    reduce_scatter x1, waiting for transfers between devices, on_device(): lax.psum_scatter(lax.dot_general(left_rows, applied, (((1,), (1,)), ((),...  60.9 us
    dot_general x1, matrix products, on_device(): jnp.dot(lax.all_gather(doc_features, 'feat', axis=1, tiled=True), inverse...  25.5 us
    dot_general x1, matrix products, on_device(): lax.dot_general(left_rows, applied, (((1,), (1,)), ((), ())), precision=l...  5.07 us
  transfers between devices with their start and end apart: 3, of which 2 were waited for; matrix products, arithmetic and copies ran while one was open for 14% of the time, Pallas kernels for 0%

commit v1 on v0

--- a/solution.py
+++ b/solution.py
@@ -4,11 +4,31 @@
 from jax.sharding import PartitionSpec as P
 
 
+def joined_along(blocks, dim):
+    lengths = list(blocks.shape[1:])
+    lengths[dim] *= blocks.shape[0]
+    return jnp.moveaxis(blocks, 0, dim).reshape(lengths)
+
+
+def collected_by_bits(shard, axis):
+    devices = lax.axis_size(axis)
+    blocks = shard[None]
+    for level in range(devices.bit_length() - 1):
+        bit = 1 << level
+        other = lax.ppermute(blocks, axis, [(i, i ^ bit) for i in range(devices)])
+        both = jnp.stack([blocks, other])
+        upper = lax.axis_index(axis) >> level & 1
+        blocks = jnp.where(upper == 0, both, both[::-1]).reshape(-1, *shard.shape)
+    return blocks
+
+
+def collect(shard, axis, dim):
+    return joined_along(collected_by_bits(shard, axis), dim)
+
+
 def on_device(query_features, inverse_kernel, doc_features):
     applied = jnp.dot(
-        lax.all_gather(doc_features, "feat", axis=1, tiled=True),
-        inverse_kernel,
-        preferred_element_type=jnp.float32,
+        collect(doc_features, "feat", 1), inverse_kernel, preferred_element_type=jnp.float32
     )
     left_rows = lax.all_gather(query_features, "corp", axis=0, tiled=True).astype(jnp.float32)
     return lax.psum_scatter(

time: 184 us -> 249 us (1.35)
  waiting for transfers between devices: 139 us -> 185 us
  other arithmetic: 0 us -> 7.58 us
  starting transfers between devices: 0.08 us -> 7.47 us
  local copies, waits for them, and re-layouts: 0.93 us -> 5.94 us
    ppermute x0 -> x3, waiting for transfers between devices: none -> 122 us  [collected_by_bits(): other = lax.ppermute(blocks, axis, [(i, i ^ bit) for i in range(devices)])]
    all_gather x1 -> x0, waiting for transfers between devices: 77 us -> none  [on_device(): lax.all_gather(doc_features, 'feat', axis=1, tiled=True)]
    ppermute x0 -> x3, starting transfers between devices: none -> 7.42 us  [collected_by_bits(): other = lax.ppermute(blocks, axis, [(i, i ^ bit) for i in range(devices)])]
    another operation x0 -> x4, other arithmetic: none -> 4.35 us  [collected_by_bits(): both = jnp.stack([blocks, other])]
    select_n x0 -> x2, other arithmetic: none -> 3.23 us  [collected_by_bits(): blocks = jnp.where(upper == 0, both, both[::-1]).reshape(-1, *shard.shape)]
    another operation x0 -> x1, local copies, waits for them, and re-layouts: none -> 2.52 us  [collected_by_bits(): both = jnp.stack([blocks, other])]
    reshape x0 -> x1, local copies, waits for them, and re-layouts: none -> 2.5 us  [collected_by_bits(): blocks = jnp.where(upper == 0, both, both[::-1]).reshape(-1, *shard.shape)]
  transfers between devices with their start and end apart: 3 -> 5, of which waited for: 2 -> 4; matrix products, arithmetic and copies ran while one was open for 14% -> 13% of each run, Pallas kernels for 0% -> 0%
where the time goes in v1:
time: 249 us; the launch traced here: 248 us
  waiting for transfers between devices  185 us (74%)
  matrix products  29.1 us (12%)
  between operations  13.5 us (5%)
  other arithmetic  7.58 us (3%)
  starting transfers between devices  7.47 us (3%)
  local copies, waits for them, and re-layouts  5.94 us (2%)
    ppermute x3, waiting for transfers between devices, collected_by_bits(): other = lax.ppermute(blocks, axis, [(i, i ^ bit) for i in range(devices)])  122 us
    reduce_scatter x1, waiting for transfers between devices, on_device(): lax.psum_scatter(lax.dot_general(left_rows, applied, (((1,), (1,)), ((),...  63.2 us
    dot_general x1, matrix products, on_device(): jnp.dot(collect(doc_features, 'feat', 1), inverse_kernel, preferred_eleme...  24 us
    ppermute x3, starting transfers between devices, collected_by_bits(): other = lax.ppermute(blocks, axis, [(i, i ^ bit) for i in range(devices)])  7.42 us
    dot_general x1, matrix products, on_device(): lax.dot_general(left_rows, applied, (((1,), (1,)), ((), ())), precision=l...  5.07 us
  transfers between devices with their start and end apart: 5, of which 4 were waited for; matrix products, arithmetic and copies ran while one was open for 13% of the time, Pallas kernels for 0%

profile of v1, /device:TPU:0, one launch (start us, length us, event | category | flops | bytes accessed | tf_op | source)
XLA Modules:
  0.0 248.3 jit_solution(10318114795731122448)
XLA Ops:
  6.5 0.0 all-gather.2.cloned.1.call-start
  6.5 3.0 %collective-permute-start = (bf16[1,128,2048]{2,1,0:T(8,128)(2,1)}, bf16[1,128,2048]{2,1,0:T(8,128)(2,1)S(1)}, u32[]{:S(2)}, u32[]{:S(2)}) collective-permute-start(bf16[1,128,2048]{2,1,0:T(8,128)(2,1)} %bitcast.27), channel_id=1, source_target_pairs={{0,2},{2,0},{4,6},{6,4},{8,10},{10,8},{12,14},{14,12},{1,3},{3,1},... | collective-permute-start | bytes 1572872 | tf_op jit(solution)/shard_map/ppermute | solution.py:18
  9.5 12.1 %collective-permute-done = bf16[1,128,2048]{2,1,0:T(8,128)(2,1)S(1)} collective-permute-done((bf16[1,128,2048]{2,1,0:T(8,128)(2,1)}, bf16[1,128,2048]{2,1,0:T(8,128)(2,1)S(1)}, u32[]{:S(2)}, u32[]{:S(2)}) %collective-permute-start) | collective-permute-done | bytes 524320 | tf_op jit(solution)/shard_map/ppermute | solution.py:18
  21.6 1.1 pad_maximum_fusion.2
  22.8 0.4 fusion.1
  23.2 1.9 collective-permute-start.1
  25.1 22.5 %collective-permute-done.1 = bf16[2,128,2048]{2,1,0:T(8,128)(2,1)S(1)} collective-permute-done((bf16[2,128,2048]{2,1,0:T(8,128)(2,1)S(1)}, bf16[2,128,2048]{2,1,0:T(8,128)(2,1)S(1)}, u32[]{:S(2)}, u32[]{:S(2)}) %collective-permute-start.1) | collective-permute-done | bytes 1048608 | tf_op jit(solution)/shard_map/ppermute | solution.py:18
  47.6 0.2 pad_maximum_fusion.1
  47.8 0.5 reverse_select_fusion.1
  48.3 2.5 %copy.8 = bf16[4,128,2048]{1,2,0:T(8,128)(2,1)} copy(bf16[4,128,2048]{2,1,0:T(8,128)(2,1)S(1)} %bitcast.23) | data formatting | bytes 4194304 | tf_op jit(solution)/shard_map/reshape | solution.py:21
  50.8 2.6 %collective-permute-start.2 = (bf16[4,128,2048]{1,2,0:T(8,128)(2,1)}, bf16[4,128,2048]{1,2,0:T(8,128)(2,1)}, u32[]{:S(2)}, u32[]{:S(2)}) collective-permute-start(bf16[4,128,2048]{1,2,0:T(8,128)(2,1)} %copy.8), channel_id=1, source_target_pairs={{0,8},{2,10},{4,12},{6,14},{8,0},{10,2},{12,4},{14,6},{1,9},{3,11}... | collective-permute-start | bytes 6291464 | tf_op jit(solution)/shard_map/ppermute | solution.py:18
  53.3 0.0 all-gather.2.cloned.1.call-update
  53.4 0.0 reduce-scatter.4.cloned.1.call-start
  53.4 2.5 %copy.9 = bf16[1,4,128,2048]{2,3,1,0:T(8,128)(2,1)} copy(bf16[1,4,128,2048]{3,2,1,0:T(8,128)(2,1)S(1)} %bitcast.24) | data formatting | bytes 4194304 | tf_op jit(solution)/shard_map/stack;reshape | solution.py:19
  55.9 86.9 %collective-permute-done.2 = bf16[4,128,2048]{1,2,0:T(8,128)(2,1)} collective-permute-done((bf16[4,128,2048]{1,2,0:T(8,128)(2,1)}, bf16[4,128,2048]{1,2,0:T(8,128)(2,1)}, u32[]{:S(2)}, u32[]{:S(2)}) %collective-permute-start.2) | collective-permute-done | bytes 2097184 | tf_op jit(solution)/shard_map/ppermute | solution.py:18
  142.9 2.6 %pad_maximum_fusion = bf16[2,4,128,2048]{2,3,1,0:T(8,128)(2,1)S(1)} fusion(bf16[1,4,128,2048]{2,3,1,0:T(8,128)(2,1)} %bitcast.8, bf16[1,4,128,2048]{2,3,1,0:T(8,128)(2,1)} %copy.9), kind=kLoop, calls=%fused_computation.1 | loop fusion | flops 2097152 | bytes 8388608 | tf_op jit(solution)/shard_map/stack | solution.py:19
  145.5 2.8 %reverse_select_fusion = bf16[2,4,128,2048]{2,3,1,0:T(8,128)(2,1)} fusion(bf16[2,4,128,2048]{2,3,1,0:T(8,128)(2,1)S(1)} %pad_maximum_fusion, pred[]{:T(512)S(6)} %eq.9), kind=kLoop, calls=%fused_computation | loop fusion | flops 2097152 | bytes 8388609 | tf_op jit(solution)/shard_map/jit(_where)/select_n | solution.py:21
  148.2 24.0 %fusion.2 = f32[128,2048]{1,0:T(8,128)S(1)} fusion(bf16[128,16384]{0,1:T(8,128)(2,1)} %bitcast.25, bf16[16384,2048]{1,0:T(8,128)(2,1)} %param.4), kind=kOutput, calls=%fused_computation.9 | convolution fusion | flops 8589934592 | bytes 72351744 | tf_op jit(solution)/shard_map/dot_general | solution.py:30
  172.2 0.0 all-gather.2.cloned.1.call-done
  172.3 5.1 %convolution_bitcast_fusion = f32[768,128]{0,1:T(8,128)S(1)} fusion(f32[128,2048]{1,0:T(8,128)S(1)} %fusion.2, bf16[768,2048]{1,0:T(8,128)(2,1)} %all-gather.2.cloned.1.call-done), kind=kOutput, calls=%fused_computation.5 | convolution fusion | flops 2415919104 | bytes 4587520 | tf_op jit(solution)/shard_map/dot_general | solution.py:35
  177.3 0.9 copy.11
  178.2 0.0 reduce-scatter.4.cloned.1.call-update
  178.3 63.2 %reduce-scatter.4.cloned.1.call-done = f32[96,128]{1,0:T(8,128)} async-done(((f32[768,128]{1,0:T(8,128)}), f32[96,128]{1,0:T(8,128)}) %reduce-scatter.4.cloned.1.call-update) | async-done | bytes 49168 | tf_op jit(solution)/shard_map/reduce_scatter | solution.py:34
Async XLA Ops:
  6.5 165.7 %all-gather.2.cloned.1.call-start = ((), (), s32[]{:S(2)}) async-start(), calls=%async_computation.1 | async-start | bytes 4718592 | tf_op jit(solution)/shard_map/all_gather | solution.py:33
  6.5 15.1 %collective-permute-start = (bf16[1,128,2048]{2,1,0:T(8,128)(2,1)}, bf16[1,128,2048]{2,1,0:T(8,128)(2,1)S(1)}, u32[]{:S(2)}, u32[]{:S(2)}) collective-permute-start(bf16[1,128,2048]{2,1,0:T(8,128)(2,1)} %bitcast.27), channel_id=1, source_target_pairs={{0,2},{2,0},{4,6},{6,4},{8,10},{10,8},{12,14},{14,12},{1,3},{3,1},... | collective-permute-start | bytes 1572872 | tf_op jit(solution)/shard_map/ppermute | solution.py:18
  23.2 24.4 %collective-permute-start.1 = (bf16[2,128,2048]{2,1,0:T(8,128)(2,1)S(1)}, bf16[2,128,2048]{2,1,0:T(8,128)(2,1)S(1)}, u32[]{:S(2)}, u32[]{:S(2)}) collective-permute-start(bf16[2,128,2048]{2,1,0:T(8,128)(2,1)S(1)} %get-tuple-element.6), channel_id=1, source_target_pairs={{0,4},{2,6},{4,0},{6,2},{8,12},{10,14},{12,8},{14,10},{1,5},{3,7},... | collective-permute-start | bytes 3145736 | tf_op jit(solution)/shard_map/ppermute | solution.py:18
  50.8 92.1 %collective-permute-start.2 = (bf16[4,128,2048]{1,2,0:T(8,128)(2,1)}, bf16[4,128,2048]{1,2,0:T(8,128)(2,1)}, u32[]{:S(2)}, u32[]{:S(2)}) collective-permute-start(bf16[4,128,2048]{1,2,0:T(8,128)(2,1)} %copy.8), channel_id=1, source_target_pairs={{0,8},{2,10},{4,12},{6,14},{8,0},{10,2},{12,4},{14,6},{1,9},{3,11}... | collective-permute-start | bytes 6291464 | tf_op jit(solution)/shard_map/ppermute | solution.py:18
  53.4 188.1 %reduce-scatter.4.cloned.1.call-start = ((), (), s32[]{:S(2)}) async-start(), calls=%async_computation.2 | async-start | bytes 442368 | tf_op jit(solution)/shard_map/reduce_scatter | solution.py:34
Sparse Core Ops, SparseCore 0:
  53.5 11.3 all-gather.1
  178.4 63.0 reduce-scatter.3
